TPU v7x, 32 devices: a whole 2x2x4 slice. The times are simulated.
32 devices in a mesh: mem: 8 (over z, x), feat: 4 (over y, core).
Axes of the slice: x: 2, y: 2, z: 4, core: 2. Of those that a mesh axis runs over, the one named last changes fastest.
Arguments:
- events: bfloat16 [2048, 32, 256], P('mem'), may hold values from -6 to 6
- w_in: bfloat16 [256, 1024], P(None, 'feat'), may hold values from -0.375 to 0.375
- w_out: bfloat16 [1024, 256], P('feat'), may hold values from -0.1875 to 0.1875
- probe_vectors: bfloat16 [2048, 256], P(('mem', 'feat')), may hold values from -8 to 8
- key_queue: bfloat16 [65536, 256], P('mem'), may hold values from -1 to 1
- target_position: int32 [2048], P(('mem', 'feat')), may hold values from 0 to 65535
- pointer: int32 [1], replicated, may hold values from 0 to 65535
Outputs:
- loss: float32 [2048], P(('mem', 'feat'))
- probe_derivative: float32 [2048, 256], P(('mem', 'feat'))
- new_memory: bfloat16 [65536, 256], P('mem')
All inputs are finite; a program needn't handle non-finite values.
Results may differ from a plain program's by a relative error of at most 0.0017.
Values may be sent and summed in bfloat16 or wider, within the bound.
A program may use at most 64 MiB of HBM per device.

v0:
```python
import jax
import jax.numpy as jnp
from jax import lax
from jax.sharding import PartitionSpec as P

inverse_softness = 14.0
epsilon = 1e-06


def normalize_keys(raw_key):
    scaled = (
        raw_key * lax.rsqrt(jnp.mean(raw_key * raw_key, axis=1, keepdims=True) + epsilon) / 16.0
    )
    return scaled.astype(jnp.bfloat16)


def slot_scores(query_rows, queue_position_span):
    similarity_entry = lax.dot_general(
        query_rows,
        queue_position_span,
        (((1,), (1,)), ((), ())),
        preferred_element_type=jnp.float32,
    )
    return similarity_entry * inverse_softness


def shards(events, w_in, w_out, probe_vectors, key_queue, target_position, pointer):
    sessions = events.shape[0]
    flattened = events.reshape(sessions * events.shape[1], events.shape[2])
    activation = jax.nn.gelu(jnp.dot(flattened, w_in, preferred_element_type=jnp.float32))
    pooled = jnp.mean(
        activation.reshape(sessions, events.shape[1], activation.shape[1]), axis=1
    ).astype(jnp.bfloat16)
    partial_key = jnp.dot(pooled, w_out, preferred_element_type=jnp.float32)
    key_whole = lax.psum(partial_key, "feat")
    keys_all = lax.all_gather(normalize_keys(key_whole), "mem", axis=0, tiled=True)
    cycle_size = key_queue.shape[0]
    slots_total = cycle_size * lax.axis_size("mem")
    cycle_first = lax.axis_index("mem") * cycle_size
    global_slot = cycle_first + jnp.arange(cycle_size, dtype=jnp.int32)
    offsets = (global_slot - pointer[0]) % slots_total
    session_count = keys_all.shape[0]
    picked = jnp.take(keys_all, jnp.minimum(offsets, session_count - 1), axis=0)
    new_memory = jnp.where((offsets < session_count)[:, None], picked, key_queue)
    gathered_queries, gathered_positive = (
        lax.all_gather(probe_vectors, "mem", axis=0, tiled=True),
        lax.all_gather(target_position, "mem", axis=0, tiled=True),
    )
    row_total = gathered_queries.shape[0]
    block_size = min(1024, cycle_size)
    block_count = cycle_size // block_size
    slot_blocks = key_queue.reshape(block_count, block_size, key_queue.shape[1])
    block_starts = jnp.arange(block_count, dtype=jnp.int32) * block_size
    positions = jnp.arange(block_size, dtype=jnp.int32)
    local_positive = gathered_positive - cycle_first

    def first_pass(carry, item):
        running_max, running_sum, positive_score = carry
        queue_position_span, first_slot = item
        similarity_table = slot_scores(gathered_queries, queue_position_span)
        new_max = jnp.maximum(running_max, jnp.max(similarity_table, axis=1))
        running_sum = running_sum * jnp.exp(running_max - new_max) + jnp.sum(
            jnp.exp(similarity_table - new_max[:, None]), axis=1
        )
        hit = positions[None, :] == (local_positive - first_slot)[:, None]
        positive_score = positive_score + jnp.sum(jnp.where(hit, similarity_table, 0.0), axis=1)
        return ((new_max, running_sum, positive_score), None)

    start_carry = (
        jnp.full((row_total,), -jnp.inf, jnp.float32),
        jnp.zeros((row_total,), jnp.float32),
        jnp.zeros((row_total,), jnp.float32),
    )
    (local_max, local_sum, local_score), stored = lax.scan(
        first_pass, start_carry, (slot_blocks, block_starts)
    )
    top = lax.pmax(local_max, "mem")
    total, positive_score = lax.psum((local_sum * jnp.exp(local_max - top), local_score), "mem")
    own_rows = probe_vectors.shape[0]
    own_first = lax.axis_index("mem") * own_rows
    loss_all = top + jnp.log(total) - positive_score
    loss = lax.dynamic_slice_in_dim(loss_all, own_first, own_rows)

    def add_weighted(collected_denominator, similarity_table, queue_position_span):
        weights = (jnp.exp(similarity_table - top[:, None]) / total[:, None]).astype(jnp.bfloat16)
        return collected_denominator + jnp.dot(
            weights, queue_position_span, preferred_element_type=jnp.float32
        )

    start_sum = jnp.zeros((lax.axis_size("mem") * own_rows, key_queue.shape[1]), jnp.float32)

    def second_pass(collected_denominator, queue_position_span):
        return (
            add_weighted(
                collected_denominator,
                slot_scores(gathered_queries, queue_position_span),
                queue_position_span,
            ),
            None,
        )

    collected_denominator, unused_part = lax.scan(second_pass, start_sum, slot_blocks)
    inside = (local_positive >= 0) & (local_positive < cycle_size)
    paired_entries = jnp.take(
        key_queue, jnp.clip(local_positive, 0, cycle_size - 1), axis=0
    ).astype(jnp.float32)
    paired_entries = jnp.where(inside[:, None], paired_entries, 0.0)
    probe_derivative = lax.psum_scatter(
        inverse_softness * (collected_denominator - paired_entries),
        "mem",
        scatter_dimension=0,
        tiled=True,
    )
    return (loss, probe_derivative, new_memory)


def solution(mesh):
    placed = (
        P("mem", None, None),
        P(None, "feat"),
        P("feat", None),
        P(("mem", "feat"), None),
        P("mem", None),
        P(("mem", "feat")),
        P(),
    )
    return jax.shard_map(
        shards,
        mesh=mesh,
        in_specs=placed,
        out_specs=(P(("mem", "feat")), P(("mem", "feat"), None), P("mem", None)),
        check_vma=False,
    )
```

profile of v0, /device:TPU:0, one launch (start us, length us, event | category | flops | bytes accessed | tf_op | source)
XLA Modules:
  0.0 237.6 jit_solution(11309458227827975150)
XLA Ops:
  7.2 0.0 all-reduce.4.cloned.1.call-start
  7.2 0.8 copy-done
  8.1 5.8 %bitcast_reduce_fusion = f32[256,256]{1,0:T(8,128)S(1)} fusion(bf16[8192,256]{1,0:T(8,128)(2,1)} %bitcast.51, bf16[256,256]{1,0:T(8,128)(2,1)S(1)} %copy-done), kind=kOutput, calls=%fused_computation.36 | convolution fusion | flops 1092550656 | bytes 4587520 | tf_op jit(solution)/shard_map/dot_general | solution.py:30
  13.9 0.9 fusion.27
  14.8 0.0 all-gather.2.cloned.1.call-start
  14.9 0.6 dynamic-slice
  16.2 0.2 dynamic-update-slice
  16.4 13.1 %all-reduce = s32[512]{0:T(512)S(1)} all-reduce(s32[512]{0:T(512)S(1)} %dynamic-update-slice), channel_id=1, replica_groups=mesh['mem'=8,'feat'=4] {'mem'}, use_global_device_ids=true, to_apply=%add | all-reduce | flops 512 | bytes 4096
  29.5 30.8 %all_gather.9 = bf16[512,256]{1,0:T(8,128)(2,1)S(1)} all-gather(bf16[64,256]{1,0:T(8,128)(2,1)S(1)} %copy-done.2), channel_id=1, replica_groups=mesh['mem'=8,'feat'=4] {'mem'}, dimensions={0}, use_global_device_ids=true | all-gather | bytes 294912 | tf_op jit(solution)/shard_map/all_gather | solution.py:46
  60.3 27.6 %while.26 = (s32[]{:T(128)}, f32[512]{0:T(512)S(1)}, f32[512]{0:T(512)S(1)}, f32[512]{0:T(512)S(1)}, bf16[8,1024,256]{2,1,0:T(8,128)(2,1)}, /*index=5*/bf16[512,...) while((s32[]{:T(128)}, f32[512]{0:T(512)S(1)}, ...), condition=%wide.region_4.5_spmd.clone, body=%wide.region_0.4_spmd.clone.sunk | while | flops 272633344 | bytes 5022336 | solution.py:74
  60.3 1.5 multiply_reduce_fusion.3
  61.8 0.6 dynamic_slice.36
  62.4 0.6 broadcast_subtract_fusion.4
  63.1 0.6 fusion.45
  63.7 1.5 multiply_reduce_fusion.3
  65.3 0.6 dynamic_slice.36
  65.9 0.6 broadcast_subtract_fusion.4
  66.5 0.6 fusion.45
  67.2 1.5 multiply_reduce_fusion.3
  68.7 0.6 dynamic_slice.36
  69.3 0.6 broadcast_subtract_fusion.4
  70.0 0.6 fusion.45
  70.6 1.5 multiply_reduce_fusion.3
  72.2 0.6 dynamic_slice.36
  72.8 0.6 broadcast_subtract_fusion.4
  73.4 0.6 fusion.45
  74.1 1.5 multiply_reduce_fusion.3
  75.6 0.6 dynamic_slice.36
  76.2 0.6 broadcast_subtract_fusion.4
  76.9 0.6 fusion.45
  77.6 1.5 multiply_reduce_fusion.3
  79.1 0.6 dynamic_slice.36
  79.7 0.6 broadcast_subtract_fusion.4
  80.3 0.6 fusion.45
  81.0 1.5 multiply_reduce_fusion.3
  82.6 0.6 dynamic_slice.36
  83.1 0.6 broadcast_subtract_fusion.4
  83.8 0.6 fusion.45
  84.5 1.5 multiply_reduce_fusion.3
  86.0 0.6 dynamic_slice.36
  86.6 0.6 broadcast_subtract_fusion.4
  87.3 0.6 fusion.45
  87.9 18.7 %pmax.7 = f32[512]{0:T(512)S(1)} all-reduce(f32[512]{0:T(512)S(1)} %get-tuple-element.84), channel_id=1, replica_groups=mesh['mem'=8,'feat'=4] {'mem'}, use_global_device_ids=true, to_apply=%region_5.6 | all-reduce | flops 512 | bytes 4096 | tf_op jit(solution)/shard_map/pmax | solution.py:77
  106.7 17.5 %all-reduce.1 = (f32[512]{0:T(512)S(1)}, f32[512]{0:T(512)S(1)}) all-reduce(f32[512]{0:T(512)S(1)} %get-tuple-element.86, f32[512]{0:T(512)S(1)} %exponential_multiply_fusion), channel_id=1, replica_groups=mesh['mem'=8,'feat'=4] {'mem'}, use_global_device_ids=true, to_apply=%region_7.8 | all-reduce | flops 1024 | bytes 8192 | tf_op jit(solution)/shard_map/psum | solution.py:78
  124.2 1.1 multiply_reduce_fusion.1
  125.3 1.7 multiply_convert_fusion
  127.0 0.0 reduce-scatter.2.cloned.1.call-start
  127.0 19.9 %while.27 = (s32[]{:T(128)}, f32[512,256]{1,0:T(8,128)S(1)}, bf16[8,1024,256]{2,1,0:T(8,128)(2,1)}, bf16[512,256]{1,0:T(8,128)(2,1)S(1)}, f32[512]{0:T(512)S(1)}, /*index=5*/f32[512]{0:T(512)S(1)}, s32[]{:T(128)}, s32[]{:T(128)}) while((s32[]{:T(128)}, f32[512,256]{1,0:T(8,128)S(1)}, bf16[8,1024,256]{2,1,0:T(8,128)(2,1)}, ...), condition=%wide.region_9.10_spmd.clone, body=%wide.region_8.9_spmd.clone.sunk | while | flops 539230208 | bytes 2364511 | solution.py:102
  127.1 2.4 %convolution_add_fusion.2 = f32[512,256]{1,0:T(8,128)S(1)} fusion(bf16[512,256]{1,0:T(8,128)(2,1)S(1)} %get-tuple-element.325, f32[512]{0:T(512)S(1)} %get-tuple-element.327, f32[512]{0:T(512)S(1)} %get-tuple-element.326, f32[512,256]{1,0:T(8,128)S(1)} %get-tuple-element.315, bf16[8,1024,256]{2,1,0:T(8,128)(2,1)} %get-tuple-element.324, ...), kind=kOutput, calls=%fused_computation.20.clone.1 | convolution fusion | flops 539230208 | bytes 2364417 | tf_op jit(solution)/shard_map/while/body/eval_jaxpr/dot_general | solution.py:86
  129.5 2.4 %convolution_add_fusion.2 = f32[512,256]{1,0:T(8,128)S(1)} fusion(bf16[512,256]{1,0:T(8,128)(2,1)S(1)} %get-tuple-element.325, f32[512]{0:T(512)S(1)} %get-tuple-element.327, f32[512]{0:T(512)S(1)} %get-tuple-element.326, f32[512,256]{1,0:T(8,128)S(1)} %get-tuple-element.315, bf16[8,1024,256]{2,1,0:T(8,128)(2,1)} %get-tuple-element.324, ...), kind=kOutput, calls=%fused_computation.20.clone.1 | convolution fusion | flops 539230208 | bytes 2364417 | tf_op jit(solution)/shard_map/while/body/eval_jaxpr/dot_general | solution.py:86
  132.0 2.5 %convolution_add_fusion.2 = f32[512,256]{1,0:T(8,128)S(1)} fusion(bf16[512,256]{1,0:T(8,128)(2,1)S(1)} %get-tuple-element.325, f32[512]{0:T(512)S(1)} %get-tuple-element.327, f32[512]{0:T(512)S(1)} %get-tuple-element.326, f32[512,256]{1,0:T(8,128)S(1)} %get-tuple-element.315, bf16[8,1024,256]{2,1,0:T(8,128)(2,1)} %get-tuple-element.324, ...), kind=kOutput, calls=%fused_computation.20.clone.1 | convolution fusion | flops 539230208 | bytes 2364417 | tf_op jit(solution)/shard_map/while/body/eval_jaxpr/dot_general | solution.py:86
  134.5 2.4 %convolution_add_fusion.2 = f32[512,256]{1,0:T(8,128)S(1)} fusion(bf16[512,256]{1,0:T(8,128)(2,1)S(1)} %get-tuple-element.325, f32[512]{0:T(512)S(1)} %get-tuple-element.327, f32[512]{0:T(512)S(1)} %get-tuple-element.326, f32[512,256]{1,0:T(8,128)S(1)} %get-tuple-element.315, bf16[8,1024,256]{2,1,0:T(8,128)(2,1)} %get-tuple-element.324, ...), kind=kOutput, calls=%fused_computation.20.clone.1 | convolution fusion | flops 539230208 | bytes 2364417 | tf_op jit(solution)/shard_map/while/body/eval_jaxpr/dot_general | solution.py:86
  137.0 2.5 %convolution_add_fusion.2 = f32[512,256]{1,0:T(8,128)S(1)} fusion(bf16[512,256]{1,0:T(8,128)(2,1)S(1)} %get-tuple-element.325, f32[512]{0:T(512)S(1)} %get-tuple-element.327, f32[512]{0:T(512)S(1)} %get-tuple-element.326, f32[512,256]{1,0:T(8,128)S(1)} %get-tuple-element.315, bf16[8,1024,256]{2,1,0:T(8,128)(2,1)} %get-tuple-element.324, ...), kind=kOutput, calls=%fused_computation.20.clone.1 | convolution fusion | flops 539230208 | bytes 2364417 | tf_op jit(solution)/shard_map/while/body/eval_jaxpr/dot_general | solution.py:86
  139.4 2.4 %convolution_add_fusion.2 = f32[512,256]{1,0:T(8,128)S(1)} fusion(bf16[512,256]{1,0:T(8,128)(2,1)S(1)} %get-tuple-element.325, f32[512]{0:T(512)S(1)} %get-tuple-element.327, f32[512]{0:T(512)S(1)} %get-tuple-element.326, f32[512,256]{1,0:T(8,128)S(1)} %get-tuple-element.315, bf16[8,1024,256]{2,1,0:T(8,128)(2,1)} %get-tuple-element.324, ...), kind=kOutput, calls=%fused_computation.20.clone.1 | convolution fusion | flops 539230208 | bytes 2364417 | tf_op jit(solution)/shard_map/while/body/eval_jaxpr/dot_general | solution.py:86
  141.9 2.5 %convolution_add_fusion.2 = f32[512,256]{1,0:T(8,128)S(1)} fusion(bf16[512,256]{1,0:T(8,128)(2,1)S(1)} %get-tuple-element.325, f32[512]{0:T(512)S(1)} %get-tuple-element.327, f32[512]{0:T(512)S(1)} %get-tuple-element.326, f32[512,256]{1,0:T(8,128)S(1)} %get-tuple-element.315, bf16[8,1024,256]{2,1,0:T(8,128)(2,1)} %get-tuple-element.324, ...), kind=kOutput, calls=%fused_computation.20.clone.1 | convolution fusion | flops 539230208 | bytes 2364417 | tf_op jit(solution)/shard_map/while/body/eval_jaxpr/dot_general | solution.py:86
  144.4 2.5 %convolution_add_fusion.2 = f32[512,256]{1,0:T(8,128)S(1)} fusion(bf16[512,256]{1,0:T(8,128)(2,1)S(1)} %get-tuple-element.325, f32[512]{0:T(512)S(1)} %get-tuple-element.327, f32[512]{0:T(512)S(1)} %get-tuple-element.326, f32[512,256]{1,0:T(8,128)S(1)} %get-tuple-element.315, bf16[8,1024,256]{2,1,0:T(8,128)(2,1)} %get-tuple-element.324, ...), kind=kOutput, calls=%fused_computation.20.clone.1 | convolution fusion | flops 539230208 | bytes 2364417 | tf_op jit(solution)/shard_map/while/body/eval_jaxpr/dot_general | solution.py:86
  146.9 4.3 %gather_fusion = bf16[512,256]{1,0:T(8,128)(2,1)S(1)} fusion(bf16[8192,256]{1,0:T(8,128)(2,1)} %bitcast.48, s32[1024]{0:T(1024)S(1)} %pad_clamp_fusion), kind=kCustom, calls=%fused_computation | custom fusion | bytes 526336 | tf_op jit(solution)/shard_map/jit(_take)/gather | solution.py:104
  151.3 1.0 subtract_multiply_fusion
  153.0 0.2 compare_select_fusion
  153.2 0.6 dynamic_slice.14
  153.8 11.9 %all-gather.2.cloned.1.call-done = bf16[2048,256]{1,0:T(8,128)(2,1)} async-done(((bf16[256,256]{1,0:T(8,128)(2,1)}), bf16[2048,256]{1,0:T(8,128)(2,1)}) %all-gather.2.cloned.1.call-update) | async-done | bytes 1048592 | tf_op jit(solution)/shard_map/all_gather | solution.py:36
  165.7 32.5 %gather_fusion.1 = bf16[8192,256]{1,0:T(8,128)(2,1)} fusion(bf16[2048,256]{1,0:T(8,128)(2,1)} %all-gather.2.cloned.1.call-done, s32[8192]{0:T(1024)S(1)} %broadcast_clamp_fusion), kind=kCustom, calls=%fused_computation.1 | custom fusion | bytes 8421376 | tf_op jit(solution)/shard_map/jit(_take)/gather | solution.py:43
  198.2 7.9 %select_select_fusion = bf16[8192,256]{1,0:T(8,128)(2,1)} fusion(bf16[8192,256]{1,0:T(8,128)(2,1)} %bitcast.49, bf16[8192,256]{1,0:T(8,128)(2,1)} %gather_fusion.1, pred[8192]{0:T(1024)(128)(4,1)S(1)} %get-tuple-element.176, pred[8192]{0:T(1024)(128)(4,1)S(1)} %get-tuple-element.177), kind=kLoop, calls=%fused_computation.37 | loop fusion | flops 4194304 | bytes 12599296 | tf_op jit(solution)/shard_map/jit(_where)/select_n | solution.py:44
  206.1 25.0 %reduce-scatter.2.cloned.1.call-done = f32[64,256]{1,0:T(8,128)} async-done(((f32[512,256]{1,0:T(8,128)}), f32[64,256]{1,0:T(8,128)}) %reduce-scatter.2.cloned.1.call-update) | async-done | bytes 65552 | tf_op jit(solution)/shard_map/reduce_scatter | solution.py:108
  (52 shorter events, 0.4 us)
Async XLA Ops:
  7.2 0.9 copy-start
  7.2 117.0 %all-reduce.4.cloned.1.call-start = ((), (), s32[]{:S(2)}) async-start(), calls=%async_computation.2 | async-start | bytes 524288 | tf_op jit(solution)/shard_map/psum | solution.py:35
  8.1 5.8 %copy-start.1 = (bf16[256,256]{1,0:T(8,128)(2,1)S(1)}, bf16[256,256]{1,0:T(8,128)(2,1)}, u32[]{:S(2)}) copy-start(bf16[256,256]{1,0:T(8,128)(2,1)} %param.13) | copy-start | bytes 393220
  8.1 6.8 %copy-start.4 = (u32[32]{0:T(128)S(1)}, u32[32]{0:T(128)}, u32[]{:S(2)}) copy-start(u32[32]{0:T(128)} %constant.115) | copy-start | bytes 388
  8.1 8.1 %copy-start.3 = (s32[64]{0:T(128)S(1)}, s32[64]{0:T(128)}, u32[]{:S(2)}) copy-start(s32[64]{0:T(128)} %param.16) | copy-start | bytes 772
  8.1 21.4 %copy-start.2 = (bf16[64,256]{1,0:T(8,128)(2,1)S(1)}, bf16[64,256]{1,0:T(8,128)(2,1)}, u32[]{:S(2)}) copy-start(bf16[64,256]{1,0:T(8,128)(2,1)} %param.14) | copy-start | bytes 98308
  14.8 150.9 %all-gather.2.cloned.1.call-start = ((), (), s32[]{:S(2)}) async-start(), calls=%async_computation.3 | async-start | bytes 1179648 | tf_op jit(solution)/shard_map/all_gather | solution.py:36
  127.0 104.1 %reduce-scatter.2.cloned.1.call-start = ((), (), s32[]{:S(2)}) async-start(), calls=%async_computation.1 | async-start | bytes 589824 | tf_op jit(solution)/shard_map/reduce_scatter | solution.py:108
Sparse Core Ops, SparseCore 0:
  14.9 34.9 all-reduce.3
  127.1 38.5 all-gather.1
  169.6 61.4 reduce-scatter.1
where the time goes:
time: 239 us; the launch traced here: 238 us
  blocking collectives  80.1 us (34%)
  local copies, waits for them, and re-layouts  43.8 us (18%)
  matrix products  38.6 us (16%)
  waiting for transfers between devices  36.9 us (15%)
  other arithmetic  22.3 us (9%)
  between operations  15.3 us (6%)
    gather x1, local copies, waits for them, and re-layouts, shards(): picked = jnp.take(keys_all, jnp.minimum(offsets, session_count - 1), axis=0)  32.5 us
    all_gather x1, blocking collectives, shards(): lax.all_gather(probe_vectors, 'mem', axis=0, tiled=True)  30.8 us
    reduce_scatter x1, waiting for transfers between devices, shards(): lax.psum_scatter(inverse_softness * (collected_denominator - paired_entri...  25 us
    dot_general x8, matrix products, add_weighted(): jnp.dot(weights, queue_position_span, preferred_element_type=jnp.float32)  19.7 us
    pmax x1, blocking collectives, shards(): top = lax.pmax(local_max, 'mem')  18.7 us
    psum x1, blocking collectives, shards(): lax.psum((local_sum * jnp.exp(local_max - top), local_score), 'mem')  17.5 us
    unnamed x1, blocking collectives  13.1 us
    dot_general x8, matrix products, slot_scores(): lax.dot_general(query_rows, queue_position_span, (((1,), (1,)), ((), ()))...  12.2 us
  transfers between devices with their start and end apart: 3, of which 2 were waited for; matrix products, arithmetic and copies ran while one was open for 40% of the time, Pallas kernels for 0%

commit v1 on v0

v1 whole, which is shorter than its diff:
```python
import functools

import jax
import jax.numpy as jnp
from jax import lax
from jax.experimental import pallas as pl
from jax.experimental.pallas import tpu as pltpu
from jax.sharding import PartitionSpec as P

inverse_softness = 14.0
epsilon = 1e-06
log2e = 1.4426950408889634
MESH = pl.DeviceIdType.MESH
ANY = pl.BlockSpec(memory_space=pl.ANY)
VMEM = pl.BlockSpec(memory_space=pltpu.VMEM)


def step_kernel(
    n, nf, per, ev_chunk, slot_block, q_chunk,
    ev_hbm, w_in_ref, w_out_ref, probe_ref, queue_hbm, target_ref,
    loss_ref, grad_ref, keys_ref,
    ev, queue, q_all, t_all, pooled, partial, part_in, pos, m_s, l_s, acc, paired,
    stat, stat_in, gout, g_in,
    ev_sem, queue_sem, q_ss, q_rs, t_ss, t_rs, p_ss, p_rs, k_ss, k_rs, y_ss, y_rs, c_ss, c_rs,
    s_ss, s_rs, g_ss, g_rs,
):
    me = lax.axis_index("mem")
    mf = lax.axis_index("feat")
    own = probe_ref.shape[0]
    rows_q = q_all.shape[0]
    slots, width = queue.shape
    ev_rows = ev.shape[0]
    n_ev, n_blk = ev_rows // ev_chunk, slots // slot_block
    sessions = pooled.shape[0]
    part_rows = sessions // nf

    def ev_copy(i):
        span = pl.ds(pl.multiple_of(i * ev_chunk, ev_chunk), ev_chunk)
        return pltpu.make_async_copy(ev_hbm.at[span], ev.at[span], ev_sem.at[i])

    def queue_copy(i):
        span = pl.ds(pl.multiple_of(i * slot_block, slot_block), slot_block)
        return pltpu.make_async_copy(queue_hbm.at[span], queue.at[span], queue_sem.at[i])

    for i in range(n_ev):
        ev_copy(i).start()
    for i in range(n_blk):
        queue_copy(i).start()

    def mem_peer(k):
        return (lax.rem(me + k, n), mf)

    def mem_from(k):
        return lax.rem(me + n - k, n)

    def feat_peer(k):
        return (me, lax.rem(mf + k, nf))

    barrier = pltpu.get_barrier_semaphore()
    for k in range(1, n):
        pl.semaphore_signal(barrier, inc=1, device_id=mem_peer(k), device_id_type=MESH)
    for k in range(1, nf):
        pl.semaphore_signal(barrier, inc=1, device_id=feat_peer(k), device_id_type=MESH)
    pl.semaphore_wait(barrier, n - 1 + nf - 1)

    def remote(src, dst, ss, rs, to):
        return pltpu.make_async_remote_copy(
            src_ref=src, dst_ref=dst, send_sem=ss, recv_sem=rs, device_id=to, device_id_type=MESH
        )

    own_span = pl.ds(pl.multiple_of(me * own, own), own)
    q_copies, t_copies = [], []
    for k in range(1, n):
        q_copies.append(remote(probe_ref, q_all.at[own_span], q_ss.at[k], q_rs.at[k], mem_peer(k)))
        t_copies.append(remote(target_ref, t_all.at[me], t_ss.at[k], t_rs.at[k], mem_peer(k)))
    for a in q_copies + t_copies:
        a.start()
    q_all[own_span, :] = probe_ref[...]
    t_all[me] = target_ref[...]

    events_of = ev_chunk // (sessions // n_ev)
    c1 = 0.7978845608028654
    c2 = c1 * 0.044715

    def encode(i, carry):
        ev_copy(i).wait()
        rows = ev[pl.ds(pl.multiple_of(i * ev_chunk, ev_chunk), ev_chunk), :]
        x = jnp.dot(rows, w_in_ref[...], preferred_element_type=jnp.float32)
        t = jnp.tanh(x * (c1 + c2 * (x * x)))
        y = x * t + x
        y = y.reshape(ev_chunk // events_of, events_of, y.shape[1])
        mean = jnp.sum(y, axis=1) * (0.5 / events_of)
        s = ev_chunk // events_of
        pooled[pl.ds(pl.multiple_of(i * s, s), s), :] = mean.astype(jnp.bfloat16)
        return carry

    lax.fori_loop(0, n_ev, encode, 0)
    partial[...] = jnp.dot(pooled[...], w_out_ref[...], preferred_element_type=jnp.float32)

    def part_span(f):
        return pl.ds(pl.multiple_of(f * part_rows, part_rows), part_rows)

    p_copies = []
    for k in range(1, nf):
        to = feat_peer(k)
        p_copies.append(
            remote(partial.at[part_span(to[1])], part_in.at[k], p_ss.at[k], p_rs.at[k], to)
        )
        p_copies[-1].start()

    for a in q_copies + t_copies:
        a.wait()

    diag = lax.broadcasted_iota(jnp.int32, (own, own), 0) == lax.broadcasted_iota(
        jnp.int32, (own, own), 1
    )
    for j in range(n):
        row = t_all[j].astype(jnp.float32)
        col = jnp.sum(jnp.where(diag, jnp.broadcast_to(row, (own, own)), 0.0), axis=1, keepdims=True)
        local = col.astype(jnp.int32) - me * slots
        pos[j * own : (j + 1) * own, :] = jnp.broadcast_to(local, (own, 128))

    m_s[...] = jnp.full(m_s.shape, -jnp.inf, jnp.float32)
    l_s[...] = jnp.zeros(l_s.shape, jnp.float32)
    acc[...] = jnp.zeros(acc.shape, jnp.float32)
    paired[...] = jnp.zeros(paired.shape, jnp.float32)
    scale2 = inverse_softness * log2e

    def attend(b, carry):
        queue_copy(b).wait()
        kb = queue[pl.ds(pl.multiple_of(b * slot_block, slot_block), slot_block), :]
        for c in range(rows_q // q_chunk):
            rs = slice(c * q_chunk, (c + 1) * q_chunk)
            s = lax.dot_general(
                q_all[rs, :], kb, (((1,), (1,)), ((), ())), preferred_element_type=jnp.float32
            )
            m_old = m_s[rs, :1]
            m_new = jnp.maximum(m_old, jnp.max(s, axis=1, keepdims=True))
            p = jnp.exp2((s - m_new) * scale2)
            alpha = jnp.exp2((m_old - m_new) * scale2)
            m_s[rs, :] = jnp.broadcast_to(m_new, (q_chunk, 128))
            l_new = l_s[rs, :1] * alpha + jnp.sum(p, axis=1, keepdims=True)
            l_s[rs, :] = jnp.broadcast_to(l_new, (q_chunk, 128))
            acc[rs, :] = acc[rs, :] * alpha + jnp.dot(
                p.astype(jnp.bfloat16), kb, preferred_element_type=jnp.float32
            )
            hit = lax.broadcasted_iota(jnp.int32, s.shape, 1) == (pos[rs, :1] - b * slot_block)
            paired[rs, :] += jnp.dot(
                jnp.where(hit, 1.0, 0.0).astype(jnp.bfloat16), kb, preferred_element_type=jnp.float32
            )
        return carry

    half = n_blk // 2
    lax.fori_loop(0, half, attend, 0)

    for a in p_copies:
        a.wait()
    raw = partial[part_span(mf), :]
    for k in range(1, nf):
        raw = raw + part_in[k]
    scaled = raw * lax.rsqrt(jnp.mean(raw * raw, axis=1, keepdims=True) + epsilon) / 16.0

    def key_span(m, f):
        return pl.ds(pl.multiple_of((m * nf + f) * part_rows, part_rows), part_rows)

    mine = key_span(me, mf)
    keys_ref[mine, :] = scaled.astype(jnp.bfloat16)

    def to_same(span, ss, rs, to):
        return remote(keys_ref.at[span], keys_ref.at[span], ss, rs, to)

    k_copies = [to_same(mine, k_ss.at[k], k_rs.at[k], mem_peer(k)) for k in range(1, n)]
    for a in k_copies:
        a.start()
    far_feat = lax.rem(mf + nf // 2, nf)
    far = (me, far_feat)
    near = (me, mf + 1 - 2 * lax.rem(mf, 2))
    y_copies = [to_same(mine, y_ss.at[0], y_rs.at[0], far)]
    c_copies = [to_same(mine, c_ss.at[0], c_rs.at[0], near)]
    y_copies[0].start()
    c_copies[0].start()

    lax.fori_loop(half, n_blk, attend, 0)

    lane = lax.broadcasted_iota(jnp.int32, m_s.shape, 1)
    pos_score = jnp.sum(q_all[...].astype(jnp.float32) * paired[...], axis=1, keepdims=True)
    packed = jnp.where(lane == 0, m_s[...], jnp.where(lane == 1, l_s[...], pos_score))
    stat[...] = packed.T[:8, :]
    s_copies = [
        remote(stat, stat_in.at[k], s_ss.at[k], s_rs.at[k], mem_peer(k)) for k in range(1, n)
    ]
    for a in s_copies:
        a.start()

    for k in range(1, n):
        k_copies[k - 1].wait_recv()
        span = key_span(mem_from(k), mf)
        y_copies.append(to_same(span, y_ss.at[k], y_rs.at[k], far))
        c_copies.append(to_same(span, c_ss.at[k], c_rs.at[k], near))
        y_copies[-1].start()
        c_copies[-1].start()

    for a in s_copies:
        a.wait()
    mine_stat = stat[...]
    top = mine_stat[0:1, :]
    for k in range(1, n):
        top = jnp.maximum(top, stat_in[k][0:1, :])
    total = mine_stat[1:2, :] * jnp.exp2((mine_stat[0:1, :] - top) * scale2)
    score = mine_stat[2:3, :]
    for k in range(1, n):
        other = stat_in[k]
        total = total + other[1:2, :] * jnp.exp2((other[0:1, :] - top) * scale2)
        score = score + other[2:3, :]
    loss_row = (top - score) * inverse_softness + jnp.log(total)
    loss = loss_row[:, :own]
    for j in range(1, n):
        loss = jnp.where(me == j, loss_row[:, j * own : (j + 1) * own], loss)
    loss_ref[...] = loss
    factor = jnp.exp2((mine_stat[0:1, :] - top) * scale2) / total
    factor = jnp.broadcast_to(factor, (128, rows_q)).T[:, :1]
    gout[...] = inverse_softness * (acc[...] * factor - paired[...])
    g_copies = []
    for k in range(1, n):
        to = mem_peer(k)
        span = pl.ds(pl.multiple_of(to[0] * own, own), own)
        g_copies.append(remote(gout.at[span], g_in.at[k], g_ss.at[k], g_rs.at[k], to))
        g_copies[-1].start()

    for k in range(n):
        y_copies[k].wait_recv()
        span = key_span(mem_from(k), far_feat)
        c_copies.append(to_same(span, c_ss.at[n + k], c_rs.at[n + k], near))
        c_copies[-1].start()

    grad = gout[own_span, :]
    for k in range(1, n):
        g_copies[k - 1].wait()
        grad = grad + g_in[k]
    grad_ref[...] = grad
    for a in k_copies + y_copies:
        a.wait_send()
    for a in c_copies:
        a.wait()


def fill_kernel(block, pad, start_ref, keys_ref, queue_ref, out_ref, rolled):
    start = start_ref[0]
    count = keys_ref.shape[0]
    first = pl.program_id(0) * block
    phase = jnp.bitwise_and(start, 15)
    local = pl.num_programs(0) * block

    @pl.when((pl.program_id(0) == 0) & (start < local) & (start + count > 0))
    def _():
        tile = 256

        for c in range(count // tile + 1):
            lo = max(c * tile - 16, 0)
            hi = min(c * tile + tile, count)
            x = keys_ref[lo:hi, :].astype(jnp.float32)
            if c == 0:
                x = jnp.concatenate([jnp.zeros((16, x.shape[1]), jnp.float32), x], axis=0)
            if c == count // tile:
                x = jnp.concatenate([x, jnp.zeros((16, x.shape[1]), jnp.float32)], axis=0)
            x = pltpu.roll(x, phase, 0)[16:, :]
            rolled[pad + c * tile : pad + c * tile + x.shape[0], :] = x.astype(jnp.bfloat16)

    inside = (first < start + count) & (first + block > start)

    @pl.when(inside)
    def _():
        at = pl.multiple_of(pad + first - (start - phase), 16)
        row = lax.broadcasted_iota(jnp.int32, (block, queue_ref.shape[1]), 0) + (first - start)
        take = (row >= 0) & (row < count)
        new = rolled[pl.ds(at, block), :].astype(jnp.float32)
        old = queue_ref[...].astype(jnp.float32)
        out_ref[...] = jnp.where(take, new, old).astype(jnp.bfloat16)

    @pl.when(jnp.logical_not(inside))
    def _():
        out_ref[...] = queue_ref[...]


def shards(events, w_in, w_out, probe_vectors, key_queue, target_position, pointer):
    n, nf = lax.axis_size("mem"), lax.axis_size("feat")
    sessions, per, depth = events.shape
    own, width = probe_vectors.shape
    slots = key_queue.shape[0]
    rows_q = own * n
    hidden = w_in.shape[1]
    flat = events.reshape(sessions * per, depth)
    ev_chunk = min(1024, flat.shape[0])
    slot_block = min(1024, slots)
    q_chunk = min(256, rows_q)
    part_rows = sessions // nf
    f32, bf16 = jnp.float32, jnp.bfloat16
    dma = pltpu.SemaphoreType.DMA
    loss, grad, keys = pl.pallas_call(
        functools.partial(step_kernel, n, nf, per, ev_chunk, slot_block, q_chunk),
        out_shape=(
            jax.ShapeDtypeStruct((1, own), f32),
            jax.ShapeDtypeStruct((own, width), f32),
            jax.ShapeDtypeStruct((sessions * n, width), bf16),
        ),
        in_specs=[ANY, VMEM, VMEM, VMEM, ANY, VMEM],
        out_specs=(VMEM, VMEM, VMEM),
        scratch_shapes=[
            pltpu.VMEM(flat.shape, bf16),
            pltpu.VMEM(key_queue.shape, bf16),
            pltpu.VMEM((rows_q, width), bf16),
            pltpu.VMEM((n, 1, own), jnp.int32),
            pltpu.VMEM((sessions, hidden), bf16),
            pltpu.VMEM((sessions, width), f32),
            pltpu.VMEM((nf, part_rows, width), f32),
            pltpu.VMEM((rows_q, 128), jnp.int32),
            pltpu.VMEM((rows_q, 128), f32),
            pltpu.VMEM((rows_q, 128), f32),
            pltpu.VMEM((rows_q, width), f32),
            pltpu.VMEM((rows_q, width), f32),
            pltpu.VMEM((8, rows_q), f32),
            pltpu.VMEM((n, 8, rows_q), f32),
            pltpu.VMEM((rows_q, width), f32),
            pltpu.VMEM((n, own, width), f32),
            dma((flat.shape[0] // ev_chunk,)),
            dma((slots // slot_block,)),
            dma((n,)), dma((n,)), dma((n,)), dma((n,)),
            dma((nf,)), dma((nf,)),
            dma((n,)), dma((n,)),
            dma((n,)), dma((n,)),
            dma((2 * n,)), dma((2 * n,)),
            dma((n,)), dma((n,)),
            dma((n,)), dma((n,)),
        ],
        compiler_params=pltpu.CompilerParams(
            collective_id=0, has_side_effects=True, vmem_limit_bytes=56 * 1024 * 1024
        ),
        name="step",
    )(flat, w_in, w_out, probe_vectors, key_queue, target_position.reshape(1, own))

    slots_total = slots * n
    start = lax.rem(pointer - lax.axis_index("mem") * slots + slots_total, slots_total)
    count = sessions * n
    start = jnp.where(start > slots_total - count, start - slots_total, start)
    block = min(1024, slots)
    new_memory = pl.pallas_call(
        functools.partial(fill_kernel, block, block),
        grid=(slots // block,),
        out_shape=jax.ShapeDtypeStruct(key_queue.shape, bf16),
        in_specs=[
            pl.BlockSpec(memory_space=pltpu.SMEM),
            VMEM,
            pl.BlockSpec((block, width), lambda i: (i, 0)),
        ],
        out_specs=pl.BlockSpec((block, width), lambda i: (i, 0)),
        scratch_shapes=[pltpu.VMEM((count + 2 * block + 16, width), bf16)],
        compiler_params=pltpu.CompilerParams(vmem_limit_bytes=32 * 1024 * 1024),
        name="fill",
    )(start, keys, key_queue)
    return (loss.reshape(own), grad, new_memory)


def solution(mesh):
    placed = (
        P("mem", None, None),
        P(None, "feat"),
        P("feat", None),
        P(("mem", "feat"), None),
        P("mem", None),
        P(("mem", "feat")),
        P(),
    )
    return jax.shard_map(
        shards,
        mesh=mesh,
        in_specs=placed,
        out_specs=(P(("mem", "feat")), P(("mem", "feat"), None), P("mem", None)),
        check_vma=False,
    )
```

time: 239 us -> 53 us (0.22)
  the two profiles are of different devices: /device:TPU:0 before, /device:TPU:12 now
where the time goes in v1:
time: 53 us; the launch traced here: 52.9 us
  Pallas kernels  49.2 us (93%)
  local copies, waits for them, and re-layouts  2.37 us (4%)
  between operations  1.33 us (3%)
    pallas_call x1, Pallas kernels, shards(): pl.pallas_call(functools.partial(step_kernel, n, nf, per, ev_chunk, slot_...  44.6 us
    pallas_call x1, Pallas kernels, shards(): pl.pallas_call(functools.partial(fill_kernel, block, block), grid=(slots...  4.59 us
    unnamed x10, local copies, waits for them, and re-layouts  2.37 us

profile of v1, /device:TPU:12, one launch (start us, length us, event | category | flops | bytes accessed | tf_op | source)
XLA Modules:
  0.0 52.9 jit_solution(14177899482754907586)
XLA Ops:
  1.3 0.0 copy-start
  1.3 44.6 %step.1 = (f32[1,64]{1,0:T(1,128)}, f32[64,256]{1,0:T(8,128)}, bf16[2048,256]{1,0:T(8,128)(2,1)}) custom-call(bf16[8192,256]{1,0:T(8,128)(2,1)} %bitcast.4, bf16[256,256]{1,0:T(8,128)(2,1)} %w_in_ref.1, bf16[256,256]{1,0:T(8,128)(2,1)} %w_out_ref.1, bf16[64,256]{1,0:T(8,128)(2,1)} %probe_ref.1, bf16[8192,256]{1,0:T(8,128)(2,1)} %queue_ref.1, s32[1,64]{1,0:T(1,128)} %bitcast.5), custom_call_target="tpu_custom_call" | custom-call | tf_op jit(solution)/shard_map/step/pallas_call | solution.py:299
  45.9 0.0 copy-done
  45.9 0.0 copy-start.1
  45.9 1.2 %copy-done.1 = bf16[2048,256]{1,0:T(8,128)(2,1)S(1)} copy-done((bf16[2048,256]{1,0:T(8,128)(2,1)S(1)}, bf16[2048,256]{1,0:T(8,128)(2,1)}, u32[]{:S(2)}) %copy-start.1) | copy-done | bytes 1048600
  47.1 0.0 copy-start.3
  47.2 0.0 copy-start.2
  47.2 4.6 %fill.1 = bf16[8192,256]{1,0:T(8,128)(2,1)} custom-call(s32[1]{0:T(128)S(6)} %select_n.4.start_ref, bf16[2048,256]{1,0:T(8,128)(2,1)S(1)} %copy-done.1, bf16[8192,256]{1,0:T(8,128)(2,1)S(1)} %copy-done), custom_call_target="tpu_custom_call" | custom-call | tf_op jit(solution)/shard_map/fill/pallas_call | solution.py:346
  51.7 0.0 copy-done.3
  51.7 0.5 copy.13
  52.3 0.0 copy-done.2
  52.3 0.6 %copy.14 = f32[64,256]{1,0:T(8,128)} copy(f32[64,256]{1,0:T(8,128)S(1)} %copy-done.2) | data formatting | bytes 131072
Async XLA Ops:
  1.3 44.6 %copy-start = (bf16[8192,256]{1,0:T(8,128)(2,1)S(1)}, bf16[8192,256]{1,0:T(8,128)(2,1)}, u32[]{:S(2)}) copy-start(bf16[8192,256]{1,0:T(8,128)(2,1)} %queue_ref.1) | copy-start | bytes 12582916
  45.9 1.2 %copy-start.1 = (bf16[2048,256]{1,0:T(8,128)(2,1)S(1)}, bf16[2048,256]{1,0:T(8,128)(2,1)}, u32[]{:S(2)}) copy-start(bf16[2048,256]{1,0:T(8,128)(2,1)} %get-tuple-element.8.keys_ref) | copy-start | bytes 3145732
  47.1 4.6 %copy-start.3 = (f32[1,64]{1,0:T(1,128)S(1)}, f32[1,64]{1,0:T(1,128)}, u32[]{:S(2)}) copy-start(f32[1,64]{1,0:T(1,128)} %get-tuple-element.6) | copy-start | bytes 772
  47.2 5.1 %copy-start.2 = (f32[64,256]{1,0:T(8,128)S(1)}, f32[64,256]{1,0:T(8,128)}, u32[]{:S(2)}) copy-start(f32[64,256]{1,0:T(8,128)} %get-tuple-element.13) | copy-start | bytes 196612

commit v2 on v1

v2 whole, which is shorter than its diff:
```python
import functools

import jax
import jax.numpy as jnp
from jax import lax
from jax.experimental import pallas as pl
from jax.experimental.pallas import tpu as pltpu
from jax.sharding import PartitionSpec as P

inverse_softness = 14.0
epsilon = 1e-06
log2e = 1.4426950408889634
MESH = pl.DeviceIdType.MESH
ANY = pl.BlockSpec(memory_space=pl.ANY)
VMEM = pl.BlockSpec(memory_space=pltpu.VMEM)
HBM = pl.BlockSpec(memory_space=pltpu.HBM)


def step_kernel(
    n, nf, ev_chunk, slot_block, q_chunk,
    ev_hbm, w_in_ref, w_out_ref, probe_ref, queue_hbm, target_ref,
    loss_ref, grad_ref, keys_ref,
    ev, queue, q_all, t_all, pooled, partial, part_in, pos, m_s, l_s, acc,
    pair_out, pair_in, stat_out, stat_in, gout, g_in,
    ev_sem, queue_sem, q_ss, q_rs, t_ss, t_rs, p_ss, p_rs, k_ss, k_rs, y_ss, y_rs, c_ss, c_rs,
    s_ss, s_rs, g_ss, g_rs, h_ss, h_rs,
):
    me = lax.axis_index("mem")
    mf = lax.axis_index("feat")
    own = probe_ref.shape[0]
    rows_q = q_all.shape[0]
    slots, width = queue.shape
    ev_rows = ev.shape[0]
    n_ev, n_blk = ev_rows // ev_chunk, slots // slot_block
    sessions = pooled.shape[0]
    part_rows = sessions // nf

    def ev_copy(i):
        span = pl.ds(pl.multiple_of(i * ev_chunk, ev_chunk), ev_chunk)
        return pltpu.make_async_copy(ev_hbm.at[span], ev.at[span], ev_sem.at[i])

    def queue_copy(i):
        span = pl.ds(pl.multiple_of(i * slot_block, slot_block), slot_block)
        return pltpu.make_async_copy(queue_hbm.at[span], queue.at[span], queue_sem.at[i])

    partner = me + 1 - 2 * lax.rem(me, 2)

    def mem_peer(k):
        return (lax.rem(me + k, n), mf)

    def feat_peer(k):
        return (me, lax.rem(mf + k, nf))

    def block_id(i):
        return lax.rem(me + n - i, n) if i % 2 == 0 else lax.rem(partner + n - (i - 1), n)

    barrier = pltpu.get_barrier_semaphore()
    for k in range(1, n):
        pl.semaphore_signal(barrier, inc=1, device_id=mem_peer(k), device_id_type=MESH)
    for k in range(1, nf):
        pl.semaphore_signal(barrier, inc=1, device_id=feat_peer(k), device_id_type=MESH)
    for i in range(n_ev):
        ev_copy(i).start()
    for i in range(n_blk):
        queue_copy(i).start()

    def own_span(m):
        return pl.ds(pl.multiple_of(m * own, own), own)

    q_all[own_span(me), :] = probe_ref[...]
    t_all[me] = target_ref[...]
    pl.semaphore_wait(barrier, n - 1 + nf - 1)

    def remote(src, dst, ss, rs, to):
        return pltpu.make_async_remote_copy(
            src_ref=src, dst_ref=dst, send_sem=ss, recv_sem=rs, device_id=to, device_id_type=MESH
        )

    t_copies = [
        remote(target_ref, t_all.at[me], t_ss.at[k], t_rs.at[k], mem_peer(k)) for k in range(1, n)
    ]
    q_copies = {
        k: remote(probe_ref, q_all.at[own_span(me)], q_ss.at[k], q_rs.at[k], mem_peer(k))
        for k in range(2, n, 2)
    }
    q_copies[1] = remote(
        probe_ref, q_all.at[own_span(me)], q_ss.at[1], q_rs.at[1], (partner, mf)
    )
    for a in q_copies.values():
        a.start()
    for a in t_copies:
        a.start()

    events_of = ev_rows // sessions
    c1 = 0.7978845608028654
    c2 = c1 * 0.044715

    def encode(i, carry):
        ev_copy(i).wait()
        rows = ev[pl.ds(pl.multiple_of(i * ev_chunk, ev_chunk), ev_chunk), :]
        x = jnp.dot(rows, w_in_ref[...], preferred_element_type=jnp.float32)
        t = jnp.tanh(x * (c1 + c2 * (x * x)))
        y = x * t + x
        y = y.reshape(ev_chunk // events_of, events_of, y.shape[1])
        mean = jnp.sum(y, axis=1) * (0.5 / events_of)
        s = ev_chunk // events_of
        pooled[pl.ds(pl.multiple_of(i * s, s), s), :] = mean.astype(jnp.bfloat16)
        return carry

    lax.fori_loop(0, n_ev, encode, 0)
    partial[...] = jnp.dot(pooled[...], w_out_ref[...], preferred_element_type=jnp.float32)

    def part_span(f):
        return pl.ds(pl.multiple_of(f * part_rows, part_rows), part_rows)

    p_copies = []
    for k in range(1, nf):
        to = feat_peer(k)
        p_copies.append(
            remote(partial.at[part_span(to[1])], part_in.at[k], p_ss.at[k], p_rs.at[k], to)
        )
        p_copies[-1].start()

    for k in range(2, n, 2):
        q_copies[k].wait_recv()
        span = own_span(block_id(k))
        q_copies[k + 1] = remote(
            q_all.at[span], q_all.at[span], q_ss.at[k + 1], q_rs.at[k + 1], (partner, mf)
        )
        q_copies[k + 1].start()
    for a in t_copies:
        a.wait()

    diag = lax.broadcasted_iota(jnp.int32, (own, own), 0) == lax.broadcasted_iota(
        jnp.int32, (own, own), 1
    )

    def as_column(row):
        wide = jnp.broadcast_to(row, (own, own))
        return jnp.sum(jnp.where(diag, wide, 0.0), axis=1, keepdims=True)

    for j in range(n):
        local = as_column(t_all[j].astype(jnp.float32)).astype(jnp.int32) - me * slots
        pos[j * own : (j + 1) * own, :] = jnp.broadcast_to(local, (own, 128))

    acc[...] = jnp.zeros(acc.shape, jnp.float32)

    def pick(b, carry):
        queue_copy(b).wait()
        kb = queue[pl.ds(pl.multiple_of(b * slot_block, slot_block), slot_block), :]
        for c in range(rows_q // q_chunk):
            rs = slice(c * q_chunk, (c + 1) * q_chunk)
            at = lax.broadcasted_iota(jnp.int32, (q_chunk, slot_block), 1)
            hit = at == (pos[rs, :1] - b * slot_block)
            acc[rs, :] += jnp.dot(
                jnp.where(hit, 1.0, 0.0).astype(jnp.bfloat16), kb, preferred_element_type=jnp.float32
            )
        return carry

    lax.fori_loop(0, n_blk, pick, 0)
    pair_out[...] = acc[...].astype(jnp.bfloat16)
    h_copies = []
    for k in range(1, n):
        to = mem_peer(k)
        h_copies.append(
            remote(pair_out.at[own_span(to[0])], pair_in.at[k], h_ss.at[k], h_rs.at[k], to)
        )
        h_copies[-1].start()

    for k in range(1, n, 2):
        q_copies[k].wait_recv()

    m_s[...] = jnp.full(m_s.shape, -jnp.inf, jnp.float32)
    l_s[...] = jnp.zeros(l_s.shape, jnp.float32)
    acc[...] = jnp.zeros(acc.shape, jnp.float32)
    scale2 = inverse_softness * log2e

    def attend(b, carry):
        kb = queue[pl.ds(pl.multiple_of(b * slot_block, slot_block), slot_block), :]
        for c in range(rows_q // q_chunk):
            rs = slice(c * q_chunk, (c + 1) * q_chunk)
            s = lax.dot_general(
                q_all[rs, :], kb, (((1,), (1,)), ((), ())), preferred_element_type=jnp.float32
            )
            m_old = m_s[rs, :1]
            m_new = jnp.maximum(m_old, jnp.max(s, axis=1, keepdims=True))
            p = jnp.exp2((s - m_new) * scale2)
            alpha = jnp.exp2((m_old - m_new) * scale2)
            m_s[rs, :] = jnp.broadcast_to(m_new, (q_chunk, 128))
            l_new = l_s[rs, :1] * alpha + jnp.sum(p, axis=1, keepdims=True)
            l_s[rs, :] = jnp.broadcast_to(l_new, (q_chunk, 128))
            acc[rs, :] = acc[rs, :] * alpha + jnp.dot(
                p.astype(jnp.bfloat16), kb, preferred_element_type=jnp.float32
            )
        return carry

    stage_a, stage_b = n_blk // 8, (5 * n_blk) // 8
    lax.fori_loop(0, stage_a, attend, 0)

    for a in p_copies:
        a.wait()
    raw = partial[part_span(mf), :]
    for k in range(1, nf):
        raw = raw + part_in[k]
    scaled = raw * lax.rsqrt(jnp.mean(raw * raw, axis=1, keepdims=True) + epsilon) / 16.0

    def key_span(m, f):
        return pl.ds(pl.multiple_of((m * nf + f) * part_rows, part_rows), part_rows)

    mine = key_span(me, mf)
    keys_ref[mine, :] = scaled.astype(jnp.bfloat16)
    far_feat = lax.rem(mf + nf // 2, nf)
    far = (me, far_feat)
    near = (me, mf + 1 - 2 * lax.rem(mf, 2))

    def to_same(span, ss, rs, i, to):
        a = remote(keys_ref.at[span], keys_ref.at[span], ss.at[i], rs.at[i], to)
        a.start()
        return a

    k_copies = {k: to_same(mine, k_ss, k_rs, k, mem_peer(k)) for k in range(2, n, 2)}
    k_copies[1] = to_same(mine, k_ss, k_rs, 1, (partner, mf))
    y_copies = {0: to_same(mine, y_ss, y_rs, 0, far)}
    c_copies = {0: to_same(mine, c_ss, c_rs, 0, near)}

    lax.fori_loop(stage_a, stage_b, attend, 0)

    for k in range(2, n, 2):
        k_copies[k].wait_recv()
        span = key_span(block_id(k), mf)
        k_copies[k + 1] = to_same(span, k_ss, k_rs, k + 1, (partner, mf))
        y_copies[k] = to_same(span, y_ss, y_rs, k, far)
        c_copies[k] = to_same(span, c_ss, c_rs, k, near)

    lax.fori_loop(stage_b, n_blk, attend, 0)

    gout[...] = acc[...].astype(jnp.bfloat16)
    g_copies = []
    for k in range(1, n):
        to = mem_peer(k)
        g_copies.append(remote(gout.at[own_span(to[0])], g_in.at[k], g_ss.at[k], g_rs.at[k], to))
        g_copies[-1].start()
    lane = lax.broadcasted_iota(jnp.int32, m_s.shape, 1)
    packed = jnp.where(lane == 0, m_s[...], l_s[...]).T
    for j in range(n):
        stat_out[j, 0:2, :] = packed[0:2, j * own : (j + 1) * own]
    s_copies = []
    for k in range(1, n):
        to = mem_peer(k)
        s_copies.append(remote(stat_out.at[to[0]], stat_in.at[k], s_ss.at[k], s_rs.at[k], to))
        s_copies[-1].start()

    for i in range(1, n, 2):
        k_copies[i].wait_recv()
        span = key_span(block_id(i), mf)
        y_copies[i] = to_same(span, y_ss, y_rs, i, far)
        c_copies[i] = to_same(span, c_ss, c_rs, i, near)

    paired = pair_out[own_span(me), :].astype(jnp.float32)
    for a in h_copies:
        a.wait()
    for k in range(1, n):
        paired = paired + pair_in[k].astype(jnp.float32)
    score = jnp.sum(probe_ref[...].astype(jnp.float32) * paired, axis=1, keepdims=True)
    score = jnp.sum(
        jnp.where(diag, jnp.broadcast_to(score, (own, own)), 0.0), axis=0, keepdims=True
    )

    order = [0] + list(range(2, n, 2)) + list(range(1, n, 2))
    for i in order:
        y_copies[i].wait_recv()
        c_copies[n + i] = to_same(key_span(block_id(i), far_feat), c_ss, c_rs, n + i, near)

    for a in s_copies:
        a.wait()
    stats = [stat_out[me]] + [stat_in[k] for k in range(1, n)]
    top = stats[0][0:1, :]
    for st in stats[1:]:
        top = jnp.maximum(top, st[0:1, :])
    powers = [jnp.exp2((st[0:1, :] - top) * scale2) for st in stats]
    total = stats[0][1:2, :] * powers[0]
    for st, w in zip(stats[1:], powers[1:]):
        total = total + st[1:2, :] * w
    loss_ref[...] = (top - score) * inverse_softness + jnp.log(total)
    grad = acc[own_span(me), :] * as_column(powers[0] / total)
    for k in range(1, n):
        g_copies[k - 1].wait()
        grad = grad + g_in[k].astype(jnp.float32) * as_column(powers[k] / total)
    grad_ref[...] = inverse_softness * (grad - paired)

    for a in list(q_copies.values()) + list(k_copies.values()) + list(y_copies.values()):
        a.wait_send()
    for a in c_copies.values():
        a.wait()


def fill_kernel(
    block, start_ref, keys_hbm, queue_ref, loss_in, grad_in,
    loss_ref, grad_ref, out_hbm,
    keys, rolled, merged, keys_sem, out_sem,
):
    start = start_ref[0]
    count = keys.shape[0]
    slots, width = queue_ref.shape
    phase = jnp.bitwise_and(start, 15)
    blocks = slots // block
    here = (start < slots) & (start + count > 0)
    keys_copy = pltpu.make_async_copy(keys_hbm, keys, keys_sem)

    @pl.when(here)
    def _():
        keys_copy.start()

    def spans(i):
        return slice(i * block, (i + 1) * block)

    def inside(i):
        return (i * block < start + count) & ((i + 1) * block > start)

    def plain(i):
        return pltpu.make_async_copy(queue_ref.at[spans(i)], out_hbm.at[spans(i)], out_sem.at[i])

    for i in range(blocks):

        @pl.when(jnp.logical_not(inside(i)))
        def _():
            plain(i).start()

    loss_ref[...] = loss_in[...]
    grad_ref[...] = grad_in[...]

    @pl.when(here)
    def _():
        keys_copy.wait()
        tile = min(256, count)
        for c in range(count // tile + 1):
            lo = max(c * tile - 16, 0)
            hi = min(c * tile + tile, count)
            x = keys[lo:hi, :].astype(jnp.float32)
            if c == 0:
                x = jnp.concatenate([jnp.zeros((16, width), jnp.float32), x], axis=0)
            if c == count // tile:
                x = jnp.concatenate([x, jnp.zeros((16, width), jnp.float32)], axis=0)
            x = pltpu.roll(x, phase, 0)[16:, :]
            at = block + c * tile
            rolled[at : at + x.shape[0], :] = x.astype(jnp.bfloat16)

    for i in range(blocks):

        @pl.when(inside(i))
        def _():
            at = pl.multiple_of(block + i * block - (start - phase), 16)
            row = lax.broadcasted_iota(jnp.int32, (block, width), 0) + (i * block - start)
            take = (row >= 0) & (row < count)
            new = rolled[pl.ds(at, block), :].astype(jnp.float32)
            old = queue_ref[spans(i), :].astype(jnp.float32)
            merged[spans(i), :] = jnp.where(take, new, old).astype(jnp.bfloat16)
            pltpu.make_async_copy(
                merged.at[spans(i)], out_hbm.at[spans(i)], out_sem.at[i]
            ).start()

    for i in range(blocks):
        plain(i).wait()


def shards(events, w_in, w_out, probe_vectors, key_queue, target_position, pointer):
    n, nf = lax.axis_size("mem"), lax.axis_size("feat")
    sessions, per, depth = events.shape
    own, width = probe_vectors.shape
    slots = key_queue.shape[0]
    rows_q = own * n
    hidden = w_in.shape[1]
    flat = events.reshape(sessions * per, depth)
    ev_chunk = min(1024, flat.shape[0])
    slot_block = min(1024, slots)
    q_chunk = min(256, rows_q)
    part_rows = sessions // nf
    f32, bf16 = jnp.float32, jnp.bfloat16
    dma = pltpu.SemaphoreType.DMA
    loss, grad, keys = pl.pallas_call(
        functools.partial(step_kernel, n, nf, ev_chunk, slot_block, q_chunk),
        out_shape=(
            jax.ShapeDtypeStruct((1, own), f32),
            jax.ShapeDtypeStruct((own, width), f32),
            jax.ShapeDtypeStruct((sessions * n, width), bf16),
        ),
        in_specs=[ANY, VMEM, VMEM, VMEM, ANY, VMEM],
        out_specs=(VMEM, VMEM, VMEM),
        scratch_shapes=[
            pltpu.VMEM(flat.shape, bf16),
            pltpu.VMEM(key_queue.shape, bf16),
            pltpu.VMEM((rows_q, width), bf16),
            pltpu.VMEM((n, 1, own), jnp.int32),
            pltpu.VMEM((sessions, hidden), bf16),
            pltpu.VMEM((sessions, width), f32),
            pltpu.VMEM((nf, part_rows, width), f32),
            pltpu.VMEM((rows_q, 128), jnp.int32),
            pltpu.VMEM((rows_q, 128), f32),
            pltpu.VMEM((rows_q, 128), f32),
            pltpu.VMEM((rows_q, width), f32),
            pltpu.VMEM((rows_q, width), bf16),
            pltpu.VMEM((n, own, width), bf16),
            pltpu.VMEM((n, 4, own), f32),
            pltpu.VMEM((n, 4, own), f32),
            pltpu.VMEM((rows_q, width), bf16),
            pltpu.VMEM((n, own, width), bf16),
            dma((flat.shape[0] // ev_chunk,)),
            dma((slots // slot_block,)),
            dma((n,)), dma((n,)), dma((n,)), dma((n,)),
            dma((nf,)), dma((nf,)),
            dma((n,)), dma((n,)),
            dma((n,)), dma((n,)),
            dma((2 * n,)), dma((2 * n,)),
            dma((n,)), dma((n,)),
            dma((n,)), dma((n,)),
            dma((n,)), dma((n,)),
        ],
        compiler_params=pltpu.CompilerParams(
            collective_id=0, has_side_effects=True, vmem_limit_bytes=56 * 1024 * 1024
        ),
        name="step",
    )(flat, w_in, w_out, probe_vectors, key_queue, target_position.reshape(1, own))

    slots_total = slots * n
    start = lax.rem(pointer - lax.axis_index("mem") * slots + slots_total, slots_total)
    count = sessions * n
    start = jnp.where(start > slots_total - count, start - slots_total, start)
    block = min(512, slots)
    loss, grad, new_memory = pl.pallas_call(
        functools.partial(fill_kernel, block),
        out_shape=(
            jax.ShapeDtypeStruct((1, own), f32),
            jax.ShapeDtypeStruct((own, width), f32),
            jax.ShapeDtypeStruct(key_queue.shape, bf16),
        ),
        in_specs=[pl.BlockSpec(memory_space=pltpu.SMEM), HBM, VMEM, VMEM, VMEM],
        out_specs=(VMEM, VMEM, HBM),
        scratch_shapes=[
            pltpu.VMEM((count, width), bf16),
            pltpu.VMEM((count + 2 * block + 16, width), bf16),
            pltpu.VMEM(key_queue.shape, bf16),
            dma,
            dma((slots // block,)),
        ],
        compiler_params=pltpu.CompilerParams(vmem_limit_bytes=61000 * 1024),
        name="fill",
    )(start, keys, key_queue, loss, grad)
    return (loss.reshape(own), grad, new_memory)


def solution(mesh):
    placed = (
        P("mem", None, None),
        P(None, "feat"),
        P("feat", None),
        P(("mem", "feat"), None),
        P("mem", None),
        P(("mem", "feat")),
        P(),
    )
    return jax.shard_map(
        shards,
        mesh=mesh,
        in_specs=placed,
        out_specs=(P(("mem", "feat")), P(("mem", "feat"), None), P("mem", None)),
        check_vma=False,
    )
```

time: 53 us -> 45 us (0.85)
  the two profiles are of different devices: /device:TPU:12 before, /device:TPU:0 now
where the time goes in v2:
time: 45 us; the launch traced here: 44.8 us
  Pallas kernels  43.5 us (97%)
  between operations  1.3 us (3%)
    pallas_call x1, Pallas kernels, shards(): pl.pallas_call(functools.partial(step_kernel, n, nf, ev_chunk, slot_block...  38.5 us
    pallas_call x1, Pallas kernels, shards(): pl.pallas_call(functools.partial(fill_kernel, block), out_shape=(jax.Shap...  4.97 us

profile of v2, /device:TPU:0, one launch (start us, length us, event | category | flops | bytes accessed | tf_op | source)
XLA Modules:
  0.0 44.8 jit_solution(12491140281449311077)
XLA Ops:
  1.3 38.5 %step.1 = (f32[1,64]{1,0:T(1,128)}, f32[64,256]{1,0:T(8,128)}, bf16[2048,256]{1,0:T(8,128)(2,1)}) custom-call(bf16[8192,256]{1,0:T(8,128)(2,1)} %bitcast.4, bf16[256,256]{1,0:T(8,128)(2,1)} %w_in_ref.1, bf16[256,256]{1,0:T(8,128)(2,1)} %w_out_ref.1, bf16[64,256]{1,0:T(8,128)(2,1)} %probe_ref.1, bf16[8192,256]{1,0:T(8,128)(2,1)} %queue_ref.1, s32[1,64]{1,0:T(1,128)} %bitcast.5), custom_call_target="tpu_custom_call" | custom-call | tf_op jit(solution)/shard_map/step/pallas_call | solution.py:380
  39.8 5.0 %fill.1 = (f32[1,64]{1,0:T(1,128)}, f32[64,256]{1,0:T(8,128)}, bf16[8192,256]{1,0:T(8,128)(2,1)}) custom-call(s32[1]{0:T(128)S(6)} %select_n.4.start_ref, bf16[2048,256]{1,0:T(8,128)(2,1)} %get-tuple-element.9.keys_hbm, bf16[8192,256]{1,0:T(8,128)(2,1)} %queue_ref.1, f32[1,64]{1,0:T(1,128)} %get-tuple-element.10.loss_in, f32[64,256]{1,0:T(8,128)} %get-tuple-element.11.grad_in), custom_call_target="tpu_custom_call" | custom-call | tf_op jit(solution)/shard_map/fill/pallas_call | solution.py:429

commit v3 on v2

--- a/solution.py
+++ b/solution.py
@@ -18,9 +18,9 @@
 
 def step_kernel(
     n, nf, ev_chunk, slot_block, q_chunk,
-    ev_hbm, w_in_ref, w_out_ref, probe_ref, queue_hbm, target_ref,
+    ev_hbm, w_in_hbm, w_out_hbm, probe_hbm, queue_hbm, target_ref,
     loss_ref, grad_ref, keys_ref,
-    ev, queue, q_all, t_all, pooled, partial, part_in, pos, m_s, l_s, acc,
+    w_in_ref, w_out_ref, probe_ref, load_sem, ev, queue, q_all, t_all, pooled, partial, part_in, pos, m_s, l_s, acc,
     pair_out, pair_in, stat_out, stat_in, gout, g_in,
     ev_sem, queue_sem, q_ss, q_rs, t_ss, t_rs, p_ss, p_rs, k_ss, k_rs, y_ss, y_rs, c_ss, c_rs,
     s_ss, s_rs, g_ss, g_rs, h_ss, h_rs,
@@ -28,6 +28,12 @@
     me = lax.axis_index("mem")
     mf = lax.axis_index("feat")
     own = probe_ref.shape[0]
+    loads = [
+        pltpu.make_async_copy(a, b, load_sem.at[i])
+        for i, (a, b) in enumerate(
+            ((probe_hbm, probe_ref), (w_in_hbm, w_in_ref), (w_out_hbm, w_out_ref))
+        )
+    ]
     rows_q = q_all.shape[0]
     slots, width = queue.shape
     ev_rows = ev.shape[0]
@@ -59,10 +65,13 @@
         pl.semaphore_signal(barrier, inc=1, device_id=mem_peer(k), device_id_type=MESH)
     for k in range(1, nf):
         pl.semaphore_signal(barrier, inc=1, device_id=feat_peer(k), device_id_type=MESH)
+    for a in loads:
+        a.start()
     for i in range(n_ev):
         ev_copy(i).start()
     for i in range(n_blk):
         queue_copy(i).start()
+    loads[0].wait()
 
     def own_span(m):
         return pl.ds(pl.multiple_of(m * own, own), own)
@@ -107,6 +116,8 @@
         pooled[pl.ds(pl.multiple_of(i * s, s), s), :] = mean.astype(jnp.bfloat16)
         return carry
 
+    loads[1].wait()
+    loads[2].wait()
     lax.fori_loop(0, n_ev, encode, 0)
     partial[...] = jnp.dot(pooled[...], w_out_ref[...], preferred_element_type=jnp.float32)
 
@@ -295,13 +306,13 @@
 
 
 def fill_kernel(
-    block, start_ref, keys_hbm, queue_ref, loss_in, grad_in,
+    block, start_ref, keys_hbm, queue_hbm, loss_in, grad_in,
     loss_ref, grad_ref, out_hbm,
-    keys, rolled, merged, keys_sem, out_sem,
+    keys, rolled, held, keys_sem, in_sem, out_sem,
 ):
     start = start_ref[0]
     count = keys.shape[0]
-    slots, width = queue_ref.shape
+    slots, width = held.shape
     phase = jnp.bitwise_and(start, 15)
     blocks = slots // block
     here = (start < slots) & (start + count > 0)
@@ -317,14 +328,20 @@
     def inside(i):
         return (i * block < start + count) & ((i + 1) * block > start)
 
-    def plain(i):
-        return pltpu.make_async_copy(queue_ref.at[spans(i)], out_hbm.at[spans(i)], out_sem.at[i])
+    def load(i):
+        return pltpu.make_async_copy(queue_hbm.at[spans(i)], held.at[spans(i)], in_sem.at[i])
+
+    def put(i):
+        return pltpu.make_async_copy(held.at[spans(i)], out_hbm.at[spans(i)], out_sem.at[i])
 
     for i in range(blocks):
+        load(i).start()
+    for i in range(blocks):
+        load(i).wait()
 
         @pl.when(jnp.logical_not(inside(i)))
         def _():
-            plain(i).start()
+            put(i).start()
 
     loss_ref[...] = loss_in[...]
     grad_ref[...] = grad_in[...]
@@ -353,14 +370,12 @@
             row = lax.broadcasted_iota(jnp.int32, (block, width), 0) + (i * block - start)
             take = (row >= 0) & (row < count)
             new = rolled[pl.ds(at, block), :].astype(jnp.float32)
-            old = queue_ref[spans(i), :].astype(jnp.float32)
-            merged[spans(i), :] = jnp.where(take, new, old).astype(jnp.bfloat16)
-            pltpu.make_async_copy(
-                merged.at[spans(i)], out_hbm.at[spans(i)], out_sem.at[i]
-            ).start()
+            old = held[spans(i), :].astype(jnp.float32)
+            held[spans(i), :] = jnp.where(take, new, old).astype(jnp.bfloat16)
+            put(i).start()
 
     for i in range(blocks):
-        plain(i).wait()
+        put(i).wait()
 
 
 def shards(events, w_in, w_out, probe_vectors, key_queue, target_position, pointer):
@@ -384,9 +399,13 @@
             jax.ShapeDtypeStruct((own, width), f32),
             jax.ShapeDtypeStruct((sessions * n, width), bf16),
         ),
-        in_specs=[ANY, VMEM, VMEM, VMEM, ANY, VMEM],
+        in_specs=[ANY, ANY, ANY, ANY, ANY, VMEM],
         out_specs=(VMEM, VMEM, VMEM),
         scratch_shapes=[
+            pltpu.VMEM(w_in.shape, bf16),
+            pltpu.VMEM(w_out.shape, bf16),
+            pltpu.VMEM(probe_vectors.shape, bf16),
+            dma((3,)),
             pltpu.VMEM(flat.shape, bf16),
             pltpu.VMEM(key_queue.shape, bf16),
             pltpu.VMEM((rows_q, width), bf16),
@@ -433,13 +452,14 @@
             jax.ShapeDtypeStruct((own, width), f32),
             jax.ShapeDtypeStruct(key_queue.shape, bf16),
         ),
-        in_specs=[pl.BlockSpec(memory_space=pltpu.SMEM), HBM, VMEM, VMEM, VMEM],
+        in_specs=[pl.BlockSpec(memory_space=pltpu.SMEM), HBM, HBM, VMEM, VMEM],
         out_specs=(VMEM, VMEM, HBM),
         scratch_shapes=[
             pltpu.VMEM((count, width), bf16),
             pltpu.VMEM((count + 2 * block + 16, width), bf16),
             pltpu.VMEM(key_queue.shape, bf16),
             dma,
+            dma((slots // block,)),
             dma((slots // block,)),
         ],
         compiler_params=pltpu.CompilerParams(vmem_limit_bytes=61000 * 1024),

time: 45 us -> 46.2 us (1.027)
  Pallas kernels: 43.5 us -> 44.6 us
    pallas_call x1, Pallas kernels: 38.5 us -> 39.2 us  [shards(): pl.pallas_call(functools.partial(step_kernel, n, nf, ev_chunk, slot_block...]
where the time goes in v3:
time: 46.2 us; the launch traced here: 45.9 us
  Pallas kernels  44.6 us (97%)
  between operations  1.3 us (3%)
    pallas_call x1, Pallas kernels, shards(): pl.pallas_call(functools.partial(step_kernel, n, nf, ev_chunk, slot_block...  39.2 us
    pallas_call x1, Pallas kernels, shards(): pl.pallas_call(functools.partial(fill_kernel, block), out_shape=(jax.Shap...  5.34 us

profile of v3, /device:TPU:0, one launch (start us, length us, event | category | flops | bytes accessed | tf_op | source)
XLA Modules:
  0.0 45.9 jit_solution(7977369009542595287)
XLA Ops:
  1.3 39.2 %step.1 = (f32[1,64]{1,0:T(1,128)}, f32[64,256]{1,0:T(8,128)}, bf16[2048,256]{1,0:T(8,128)(2,1)}) custom-call(bf16[8192,256]{1,0:T(8,128)(2,1)} %bitcast.4, bf16[256,256]{1,0:T(8,128)(2,1)} %w_in_hbm.1, bf16[256,256]{1,0:T(8,128)(2,1)} %w_out_hbm.1, bf16[64,256]{1,0:T(8,128)(2,1)} %probe_hbm.1, bf16[8192,256]{1,0:T(8,128)(2,1)} %queue_hbm.3, s32[1,64]{1,0:T(1,128)} %bitcast.5), custom_call_target="tpu_custom_call" | custom-call | tf_op jit(solution)/shard_map/step/pallas_call | solution.py:395
  40.5 5.3 %fill.1 = (f32[1,64]{1,0:T(1,128)}, f32[64,256]{1,0:T(8,128)}, bf16[8192,256]{1,0:T(8,128)(2,1)}) custom-call(s32[1]{0:T(128)S(6)} %select_n.4.start_ref, bf16[2048,256]{1,0:T(8,128)(2,1)} %get-tuple-element.9.keys_hbm, bf16[8192,256]{1,0:T(8,128)(2,1)} %queue_hbm.3, f32[1,64]{1,0:T(1,128)} %get-tuple-element.10.loss_in, f32[64,256]{1,0:T(8,128)} %get-tuple-element.11.grad_in), custom_call_target="tpu_custom_call" | custom-call | tf_op jit(solution)/shard_map/fill/pallas_call | solution.py:448

commit v4 on v2

--- a/solution.py
+++ b/solution.py
@@ -442,7 +442,7 @@
             dma,
             dma((slots // block,)),
         ],
-        compiler_params=pltpu.CompilerParams(vmem_limit_bytes=61000 * 1024),
+        compiler_params=pltpu.CompilerParams(vmem_limit_bytes=32 * 1024 * 1024),
         name="fill",
     )(start, keys, key_queue, loss, grad)
     return (loss.reshape(own), grad, new_memory)

time: 45 us -> 45.8 us (1.018)
  local copies, waits for them, and re-layouts: 0 us -> 2.69 us
  Pallas kernels: 43.5 us -> 41.5 us
    unnamed x0 -> x8, local copies, waits for them, and re-layouts: none -> 2.69 us
    pallas_call x1, Pallas kernels: 4.97 us -> 2.77 us  [shards(): pl.pallas_call(functools.partial(fill_kernel, block), out_shape=(jax.Shap...]
where the time goes in v4:
time: 45.8 us; the launch traced here: 45.5 us
  Pallas kernels  41.5 us (91%)
  local copies, waits for them, and re-layouts  2.69 us (6%)
  between operations  1.33 us (3%)
    pallas_call x1, Pallas kernels, shards(): pl.pallas_call(functools.partial(step_kernel, n, nf, ev_chunk, slot_block...  38.7 us
    pallas_call x1, Pallas kernels, shards(): pl.pallas_call(functools.partial(fill_kernel, block), out_shape=(jax.Shap...  2.77 us
    unnamed x8, local copies, waits for them, and re-layouts  2.69 us

profile of v4, /device:TPU:0, one launch (start us, length us, event | category | flops | bytes accessed | tf_op | source)
XLA Modules:
  0.0 45.5 jit_solution(17569423046263677964)
XLA Ops:
  1.3 0.0 copy-start
  1.3 38.7 %step.1 = (f32[1,64]{1,0:T(1,128)}, f32[64,256]{1,0:T(8,128)}, bf16[2048,256]{1,0:T(8,128)(2,1)}) custom-call(bf16[8192,256]{1,0:T(8,128)(2,1)} %bitcast.4, bf16[256,256]{1,0:T(8,128)(2,1)} %w_in_ref.1, bf16[256,256]{1,0:T(8,128)(2,1)} %w_out_ref.1, bf16[64,256]{1,0:T(8,128)(2,1)} %probe_ref.1, bf16[8192,256]{1,0:T(8,128)(2,1)} %queue_ref.1, s32[1,64]{1,0:T(1,128)} %bitcast.5), custom_call_target="tpu_custom_call" | custom-call | tf_op jit(solution)/shard_map/step/pallas_call | solution.py:380
  40.0 0.0 copy-done
  40.0 0.0 copy-start.1
  40.0 1.2 %copy-done.1 = bf16[2048,256]{1,0:T(8,128)(2,1)S(1)} copy-done((bf16[2048,256]{1,0:T(8,128)(2,1)S(1)}, bf16[2048,256]{1,0:T(8,128)(2,1)}, u32[]{:S(2)}) %copy-start.1) | copy-done | bytes 1048600
  41.2 0.0 copy-start.2
  41.2 0.8 %copy-done.2 = f32[64,256]{1,0:T(8,128)S(1)} copy-done((f32[64,256]{1,0:T(8,128)S(1)}, f32[64,256]{1,0:T(8,128)}, u32[]{:S(2)}) %copy-start.2) | copy-done | bytes 65560
  42.1 0.0 copy-start.3
  42.1 0.6 %copy-done.3 = f32[1,64]{1,0:T(1,128)S(1)} copy-done((f32[1,64]{1,0:T(1,128)S(1)}, f32[1,64]{1,0:T(1,128)}, u32[]{:S(2)}) %copy-start.3) | copy-done | bytes 280
  42.7 2.8 %fill.1 = (f32[1,64]{1,0:T(1,128)}, f32[64,256]{1,0:T(8,128)}, bf16[8192,256]{1,0:T(8,128)(2,1)}) custom-call(s32[1]{0:T(128)S(6)} %select_n.4.start_ref, bf16[2048,256]{1,0:T(8,128)(2,1)S(1)} %copy-done.1, bf16[8192,256]{1,0:T(8,128)(2,1)S(1)} %copy-done, f32[1,64]{1,0:T(1,128)S(1)} %copy-done.3, f32[64,256]{1,0:T(8,128)S(1)} %copy-done.2), custom_call_target="tpu_custom_call" | custom-call | tf_op jit(solution)/shard_map/fill/pallas_call | solution.py:429
Async XLA Ops:
  1.3 38.7 %copy-start = (bf16[8192,256]{1,0:T(8,128)(2,1)S(1)}, bf16[8192,256]{1,0:T(8,128)(2,1)}, u32[]{:S(2)}) copy-start(bf16[8192,256]{1,0:T(8,128)(2,1)} %queue_ref.1) | copy-start | bytes 12582916
  40.0 1.2 %copy-start.1 = (bf16[2048,256]{1,0:T(8,128)(2,1)S(1)}, bf16[2048,256]{1,0:T(8,128)(2,1)}, u32[]{:S(2)}) copy-start(bf16[2048,256]{1,0:T(8,128)(2,1)} %get-tuple-element.9.keys_hbm) | copy-start | bytes 3145732
  41.2 0.8 %copy-start.2 = (f32[64,256]{1,0:T(8,128)S(1)}, f32[64,256]{1,0:T(8,128)}, u32[]{:S(2)}) copy-start(f32[64,256]{1,0:T(8,128)} %get-tuple-element.11.grad_in) | copy-start | bytes 196612
  42.1 0.6 %copy-start.3 = (f32[1,64]{1,0:T(1,128)S(1)}, f32[1,64]{1,0:T(1,128)}, u32[]{:S(2)}) copy-start(f32[1,64]{1,0:T(1,128)} %get-tuple-element.10.loss_in) | copy-start | bytes 772
